TPU v7x, 256 devices: a whole 4x4x8 slice. The times are simulated.
256 devices in a mesh: cohort: 32 (over z, y), feat: 8 (over x, core).
Axes of the slice: x: 4, y: 4, z: 8, core: 2. Of those that a mesh axis runs over, the one named last changes fastest.
Arguments:
- b_factors: float32 [128, 8192, 256], P('cohort', 'feat'), may hold values from -0.375 to 0.375
- a_factors: float32 [128, 256, 8192], P('cohort', None, 'feat'), may hold values from -0.0625 to 0.0625
- ranks: int32 [128], P('cohort'), may hold values from 8 to 256, as said below
- probes: float32 [8192, 256], P('feat'), may hold values from -6 to 6
Outputs:
- subspace: float32 [8192, 256], P('feat')
Inputs may be any that keep to these rules, and one draw needn't show every extreme that they name: `ranks`: each client's rank is 8 times a power of two; some client has rank 256 and some client has rank 8.
All inputs are finite; a program needn't handle non-finite values.
Results may differ from a plain program's by a relative error of at most 0.00011.
Values sent between devices are 32-bit elements; how exact they have to be, the bound alone decides.
A program may use at most 64 MiB of HBM per device.

v0:
```python
import math

import jax
import jax.numpy as jnp
from jax import lax
from jax.sharding import PartitionSpec as P

D = 8192
ITERS = 2
NS_STEPS = 5


def product(left, right):
    return jnp.dot(left, right, precision=lax.Precision.HIGHEST, preferred_element_type=jnp.float32)


def coef_terms(a_factors, basis):
    return jnp.einsum(
        "crd,dp->crp",
        a_factors,
        basis,
        precision=lax.Precision.HIGHEST,
        preferred_element_type=jnp.float32,
    )


def panel_terms(b_factors, coef):
    return jnp.einsum(
        "cdr,crp->dp",
        b_factors,
        coef,
        precision=lax.Precision.HIGHEST,
        preferred_element_type=jnp.float32,
    )


def newton(panel, first_total, step_total):
    gram = first_total(product(panel.T, panel))
    scale = lax.rsqrt(jnp.trace(gram))
    iterate = panel * scale
    inner = gram * (scale * scale)
    for turn in range(NS_STEPS):
        iterate = 1.5 * iterate - 0.5 * product(iterate, inner)
        if turn + 1 < NS_STEPS:
            inner = step_total(product(iterate.T, iterate))
    return iterate


def feat_first(gram_part):
    return lax.psum(gram_part, "feat")


def feat_step(gram_part):
    return lax.psum(gram_part, "feat")


def on_device(b_factors, a_factors, ranks, probes):
    slots = jnp.arange(b_factors.shape[2], dtype=jnp.int32)
    live = (slots[None, :] < ranks[:, None]).astype(jnp.float32)
    basis = probes
    for turn in range(ITERS):
        coef_part = coef_terms(a_factors, basis)
        coef = lax.psum(coef_part, "feat") * live[:, :, None]
        panel_part = panel_terms(b_factors, coef)
        panel = lax.psum(panel_part, "cohort")
        basis = newton(panel, feat_first, feat_step)
    return math.sqrt(D) * basis


def solution(mesh):
    in_specs = (P("cohort", "feat", None), P("cohort", None, "feat"), P("cohort"), P("feat", None))
    out_specs = P("feat", None)
    return jax.shard_map(
        on_device, mesh=mesh, in_specs=in_specs, out_specs=out_specs, check_vma=False
    )
```

profile of v0, /device:TPU:1, one launch (start us, length us, event | category | flops | bytes accessed | tf_op | source)
XLA Modules:
  0.0 1171.2 jit_solution(10317003842640052127)
XLA Ops:
  7.8 6.9 fusion.12
  14.8 69.5 %all-reduce.15.cloned.1.call-done = f32[4,256,256]{1,2,0:T(8,128)} async-done(((f32[4,256,256]{1,2,0:T(8,128)}), f32[4,256,256]{1,2,0:T(8,128)}) %all-reduce.15.cloned.1.call-update) | async-done | bytes 1048592 | tf_op jit(solution)/shard_map/psum | solution.py:63
  84.3 7.2 convolution_bitcast_fusion.2
  91.5 147.2 %all-reduce.17.cloned.1.call-done = f32[1024,256]{0,1:T(8,128)} async-done(((f32[1024,256]{0,1:T(8,128)}), f32[1024,256]{0,1:T(8,128)}) %all-reduce.17.cloned.1.call-update) | async-done | bytes 1048592 | tf_op jit(solution)/shard_map/psum | solution.py:65
  238.7 3.3 fusion.27
  242.0 65.4 %all-reduce.19.cloned.1.call-done = f32[256,256]{1,0:T(8,128)} async-done(((f32[256,256]{1,0:T(8,128)}), f32[256,256]{1,0:T(8,128)}) %all-reduce.19.cloned.1.call-update) | async-done | bytes 262160 | tf_op jit(solution)/shard_map/psum | solution.py:50
  309.7 2.9 fusion.11
  314.5 64.4 %all-reduce.21.cloned.1.call-done = f32[256,256]{1,0:T(8,128)} async-done(((f32[256,256]{1,0:T(8,128)}), f32[256,256]{1,0:T(8,128)}) %all-reduce.21.cloned.1.call-update) | async-done | bytes 262160 | tf_op jit(solution)/shard_map/psum | solution.py:54
  378.9 2.1 fusion.10
  381.1 1.7 fusion.29
  382.9 64.6 %all-reduce.23.cloned.1.call-done = f32[256,256]{1,0:T(8,128)} async-done(((f32[256,256]{1,0:T(8,128)}), f32[256,256]{1,0:T(8,128)}) %all-reduce.23.cloned.1.call-update) | async-done | bytes 262160 | tf_op jit(solution)/shard_map/psum | solution.py:54
  447.5 2.1 fusion.9
  449.6 1.7 fusion.30
  451.4 64.6 %all-reduce.25.cloned.1.call-done = f32[256,256]{1,0:T(8,128)} async-done(((f32[256,256]{1,0:T(8,128)}), f32[256,256]{1,0:T(8,128)}) %all-reduce.25.cloned.1.call-update) | async-done | bytes 262160 | tf_op jit(solution)/shard_map/psum | solution.py:54
  516.0 2.1 fusion.8
  519.9 64.6 %all-reduce.27.cloned.1.call-done = f32[256,256]{1,0:T(8,128)} async-done(((f32[256,256]{1,0:T(8,128)}), f32[256,256]{1,0:T(8,128)}) %all-reduce.27.cloned.1.call-update) | async-done | bytes 262160 | tf_op jit(solution)/shard_map/psum | solution.py:54
  584.5 2.1 fusion.7
  586.6 6.9 convolution_bitcast_fusion.1
  593.7 66.8 %all-reduce.29.cloned.1.call-done = f32[4,256,256]{1,2,0:T(8,128)} async-done(((f32[4,256,256]{1,2,0:T(8,128)}), f32[4,256,256]{1,2,0:T(8,128)}) %all-reduce.29.cloned.1.call-update) | async-done | bytes 1048592 | tf_op jit(solution)/shard_map/psum | solution.py:63
  660.5 7.2 convolution_bitcast_fusion
  667.7 147.2 %all-reduce.31.cloned.1.call-done = f32[1024,256]{0,1:T(8,128)} async-done(((f32[1024,256]{0,1:T(8,128)}), f32[1024,256]{0,1:T(8,128)}) %all-reduce.31.cloned.1.call-update) | async-done | bytes 1048592 | tf_op jit(solution)/shard_map/psum | solution.py:65
  814.9 3.3 fusion.32
  818.3 65.4 %all-reduce.33.cloned.1.call-done = f32[256,256]{1,0:T(8,128)} async-done(((f32[256,256]{1,0:T(8,128)}), f32[256,256]{1,0:T(8,128)}) %all-reduce.33.cloned.1.call-update) | async-done | bytes 262160 | tf_op jit(solution)/shard_map/psum | solution.py:50
  885.9 2.9 fusion.5
  890.6 64.6 %all-reduce.35.cloned.1.call-done = f32[256,256]{1,0:T(8,128)} async-done(((f32[256,256]{1,0:T(8,128)}), f32[256,256]{1,0:T(8,128)}) %all-reduce.35.cloned.1.call-update) | async-done | bytes 262160 | tf_op jit(solution)/shard_map/psum | solution.py:54
  955.2 2.1 fusion.4
  959.1 64.6 %all-reduce.37.cloned.1.call-done = f32[256,256]{1,0:T(8,128)} async-done(((f32[256,256]{1,0:T(8,128)}), f32[256,256]{1,0:T(8,128)}) %all-reduce.37.cloned.1.call-update) | async-done | bytes 262160 | tf_op jit(solution)/shard_map/psum | solution.py:54
  1023.7 2.1 fusion.3
  1027.9 64.3 %all-reduce.39.cloned.1.call-done = f32[256,256]{1,0:T(8,128)} async-done(((f32[256,256]{1,0:T(8,128)}), f32[256,256]{1,0:T(8,128)}) %all-reduce.39.cloned.1.call-update) | async-done | bytes 262160 | tf_op jit(solution)/shard_map/psum | solution.py:54
  1092.2 2.1 fusion.2
  1096.1 64.6 %all-reduce.41.cloned.1.call-done = f32[256,256]{1,0:T(8,128)} async-done(((f32[256,256]{1,0:T(8,128)}), f32[256,256]{1,0:T(8,128)}) %all-reduce.41.cloned.1.call-update) | async-done | bytes 262160 | tf_op jit(solution)/shard_map/psum | solution.py:54
  1160.7 2.2 fusion.1
  (42 shorter events, 17.6 us)
Async XLA Ops:
  6.5 1.2 copy-start
  6.5 8.2 copy-start.1
  6.5 77.8 %all-reduce.15.cloned.1.call-start = ((), (), s32[]{:S(2)}) async-start(), calls=%async_computation | async-start | bytes 2097152 | tf_op jit(solution)/shard_map/psum | solution.py:63
  14.7 224.0 %all-reduce.17.cloned.1.call-start = ((), (), s32[]{:S(2)}) async-start(), calls=%async_computation.1 | async-start | bytes 2097152 | tf_op jit(solution)/shard_map/psum | solution.py:65
  91.5 215.9 %all-reduce.19.cloned.1.call-start = ((), (), s32[]{:S(2)}) async-start(), calls=%async_computation.2 | async-start | bytes 524288 | tf_op jit(solution)/shard_map/psum | solution.py:50
  242.0 137.0 %all-reduce.21.cloned.1.call-start = ((), (), s32[]{:S(2)}) async-start(), calls=%async_computation.3 | async-start | bytes 524288 | tf_op jit(solution)/shard_map/psum | solution.py:54
  314.3 133.1 %all-reduce.23.cloned.1.call-start = ((), (), s32[]{:S(2)}) async-start(), calls=%async_computation.4 | async-start | bytes 524288 | tf_op jit(solution)/shard_map/psum | solution.py:54
  382.8 133.1 %all-reduce.25.cloned.1.call-start = ((), (), s32[]{:S(2)}) async-start(), calls=%async_computation.5 | async-start | bytes 524288 | tf_op jit(solution)/shard_map/psum | solution.py:54
  451.3 133.1 %all-reduce.27.cloned.1.call-start = ((), (), s32[]{:S(2)}) async-start(), calls=%async_computation.6 | async-start | bytes 524288 | tf_op jit(solution)/shard_map/psum | solution.py:54
  519.8 140.7 %all-reduce.29.cloned.1.call-start = ((), (), s32[]{:S(2)}) async-start(), calls=%async_computation.7 | async-start | bytes 2097152 | tf_op jit(solution)/shard_map/psum | solution.py:63
  593.5 221.4 %all-reduce.31.cloned.1.call-start = ((), (), s32[]{:S(2)}) async-start(), calls=%async_computation.8 | async-start | bytes 2097152 | tf_op jit(solution)/shard_map/psum | solution.py:65
  667.7 215.9 %all-reduce.33.cloned.1.call-start = ((), (), s32[]{:S(2)}) async-start(), calls=%async_computation.9 | async-start | bytes 524288 | tf_op jit(solution)/shard_map/psum | solution.py:50
  818.2 137.0 %all-reduce.35.cloned.1.call-start = ((), (), s32[]{:S(2)}) async-start(), calls=%async_computation.10 | async-start | bytes 524288 | tf_op jit(solution)/shard_map/psum | solution.py:54
  890.6 133.1 %all-reduce.37.cloned.1.call-start = ((), (), s32[]{:S(2)}) async-start(), calls=%async_computation.11 | async-start | bytes 524288 | tf_op jit(solution)/shard_map/psum | solution.py:54
  959.1 133.1 %all-reduce.39.cloned.1.call-start = ((), (), s32[]{:S(2)}) async-start(), calls=%async_computation.12 | async-start | bytes 524288 | tf_op jit(solution)/shard_map/psum | solution.py:54
  1027.6 133.1 %all-reduce.41.cloned.1.call-start = ((), (), s32[]{:S(2)}) async-start(), calls=%async_computation.13 | async-start | bytes 524288 | tf_op jit(solution)/shard_map/psum | solution.py:54
Sparse Core Ops, SparseCore 0:
  14.8 69.4 all-reduce.14
  91.6 147.0 all-reduce.16
  242.1 65.2 all-reduce.18
  314.4 64.4 all-reduce.20
  382.9 64.4 all-reduce.22
  451.5 64.4 all-reduce.24
  520.0 64.4 all-reduce.26
  593.6 66.8 all-reduce.28
  667.8 147.0 all-reduce.30
  818.3 65.2 all-reduce.32
  890.7 64.4 all-reduce.34
  959.2 64.4 all-reduce.36
  1027.7 64.4 all-reduce.38
  1096.2 64.4 all-reduce.40
where the time goes:
time: 1180 us; the launch traced here: 1170 us
  waiting for transfers between devices  1080 us (92%)
  matrix products  71.2 us (6%)
  between operations  15.2 us (1%)
    psum x8, waiting for transfers between devices, feat_step(): return lax.psum(gram_part, 'feat')  516 us
    psum x2, waiting for transfers between devices, on_device(): panel = lax.psum(panel_part, 'cohort')  294 us
    psum x2, waiting for transfers between devices, on_device(): coef = lax.psum(coef_part, 'feat') * live[:, :, None]  136 us
    psum x2, waiting for transfers between devices, feat_first(): return lax.psum(gram_part, 'feat')  131 us
    dot_general x20, matrix products, product(): jnp.dot(left, right, precision=lax.Precision.HIGHEST, preferred_element_t...  43.1 us
  transfers between devices with their start and end apart: 14, of which 14 were waited for; matrix products, arithmetic and copies ran while one was open for 0% of the time, Pallas kernels for 0%

commit v1 on v0

v1 whole, which is shorter than its diff:
```python
import math

import jax
import jax.numpy as jnp
from jax import lax
from jax.sharding import PartitionSpec as P

D = 8192
NS_STEPS = 5


def small(left, right):
    return jnp.dot(left, right, precision=lax.Precision.HIGHEST, preferred_element_type=jnp.float32)


def big(spec, left, right):
    return jnp.einsum(
        spec, left, right, precision=lax.Precision.HIGH, preferred_element_type=jnp.float32
    )


def newton(gram):
    eye = jnp.eye(gram.shape[0], dtype=jnp.float32)
    total = None
    for turn in range(NS_STEPS):
        step = 1.5 * eye - 0.5 * gram
        total = step if total is None else small(total, step)
        if turn + 1 < NS_STEPS:
            gram = small(small(gram, step), step)
    return total


def on_device(b_factors, a_factors, ranks, probes):
    slots = jnp.arange(b_factors.shape[2], dtype=jnp.int32)
    live = (slots[None, :] < ranks[:, None]).astype(jnp.float32)[:, :, None]
    coef = lax.psum(big("crd,dp->crp", a_factors, probes), "feat") * live
    first = lax.psum(big("cdr,crp->dp", b_factors, coef), "cohort")
    gram_one = lax.psum(big("dp,dq->pq", first, first), "feat")
    coef = lax.psum(big("crd,dp->crp", a_factors, first), "feat") * live
    scale_one = lax.rsqrt(jnp.trace(gram_one))
    coef = coef * scale_one
    second = lax.psum(big("cdr,crp->dp", b_factors, coef), "cohort")
    turn_one = newton(gram_one * (scale_one * scale_one))
    gram_two = lax.psum(big("dp,dq->pq", second, second), "feat")
    gram_two = small(small(turn_one, gram_two), turn_one)
    scale_two = lax.rsqrt(jnp.trace(gram_two))
    turn_two = newton(gram_two * (scale_two * scale_two))
    turn = small(turn_one, turn_two) * (scale_two * math.sqrt(D))
    return big("dp,pq->dq", second, turn)


def solution(mesh):
    in_specs = (P("cohort", "feat", None), P("cohort", None, "feat"), P("cohort"), P("feat", None))
    out_specs = P("feat", None)
    return jax.shard_map(
        on_device, mesh=mesh, in_specs=in_specs, out_specs=out_specs, check_vma=False
    )
```

time: 1180 us -> 558 us (0.47)
  waiting for transfers between devices: 1080 us -> 495 us
  matrix products: 71.2 us -> 44.2 us
    psum x14 -> x5, waiting for transfers between devices: 1080 us -> 495 us  [the longest x1 147 us: on_device(): first = lax.psum(big('cdr,crp->dp', b_factors, coef), 'cohort')]
    dot_general x24 -> x34, matrix products: 71.2 us -> 44.2 us  [the longest x7 28.9 us: big(): jnp.einsum(spec, left, right, precision=lax.Precision.HIGH, preferred_ele...]
  transfers between devices with their start and end apart: 14 -> 5, of which waited for: 14 -> 5; matrix products, arithmetic and copies ran while one was open for 0% -> 1% of each run, Pallas kernels for 0% -> 0%
where the time goes in v1:
time: 558 us; the launch traced here: 557 us
  waiting for transfers between devices  495 us (89%)
  matrix products  44.2 us (8%)
  between operations  14.8 us (3%)
    psum x1, waiting for transfers between devices, on_device(): first = lax.psum(big('cdr,crp->dp', b_factors, coef), 'cohort')  147 us
    psum x1, waiting for transfers between devices, on_device(): second = lax.psum(big('cdr,crp->dp', b_factors, coef), 'cohort')  144 us
    psum x1, waiting for transfers between devices, on_device(): coef = lax.psum(big('crd,dp->crp', a_factors, probes), 'feat') * live  69.5 us
    psum x1, waiting for transfers between devices, on_device(): coef = lax.psum(big('crd,dp->crp', a_factors, first), 'feat') * live  68.6 us
    psum x1, waiting for transfers between devices, on_device(): gram_two = lax.psum(big('dp,dq->pq', second, second), 'feat')  65 us
    dot_general x7, matrix products, big(): jnp.einsum(spec, left, right, precision=lax.Precision.HIGH, preferred_ele...  28.9 us
    dot_general x27, matrix products, small(): jnp.dot(left, right, precision=lax.Precision.HIGHEST, preferred_element_t...  15.4 us
  transfers between devices with their start and end apart: 5, of which 5 were waited for; matrix products, arithmetic and copies ran while one was open for 1% of the time, Pallas kernels for 0%

profile of v1, /device:TPU:1, one launch (start us, length us, event | category | flops | bytes accessed | tf_op | source)
XLA Modules:
  0.0 556.9 jit_solution(10475617584359118508)
XLA Ops:
  6.5 1.2 copy-done
  7.8 5.0 fusion.3
  12.9 69.5 %all-reduce.7.cloned.1.call-done = f32[4,256,256]{1,2,0:T(8,128)} async-done(((f32[4,256,256]{1,2,0:T(8,128)}), f32[4,256,256]{1,2,0:T(8,128)}) %all-reduce.7.cloned.1.call-update) | async-done | bytes 1048592 | tf_op jit(solution)/shard_map/psum | solution.py:36
  82.4 5.4 convolution_bitcast_fusion.2
  87.8 147.2 %all-reduce.9.cloned.1.call-done = f32[1024,256]{0,1:T(8,128)} async-done(((f32[1024,256]{0,1:T(8,128)}), f32[1024,256]{0,1:T(8,128)}) %all-reduce.9.cloned.1.call-update) | async-done | bytes 1048592 | tf_op jit(solution)/shard_map/psum | solution.py:37
  235.0 2.9 fusion.176
  237.9 5.4 convolution_bitcast_fusion.1
  243.3 68.6 %all-reduce.15.cloned.1.call-done = (f32[4,256,256]{1,2,0:T(8,128)}, f32[256,256]{1,0:T(8,128)}) async-done(((f32[4,256,256]{1,2,0:T(8,128)}, f32[256,256]{1,0:T(8,128)}), (f32[4,256,256]{1,2,0:T(8,128)}, f32[256,256]{1,0:T(8,128)})) %all-reduce.15.cloned.1.call-update) | async-done | bytes 1310736 | tf_op jit(solution)/shard_map/psum | solution.py:39
  312.0 1.6 select_reduce_fusion.1
  314.3 1.5 fusion.17
  315.8 1.4 fusion.16
  317.1 1.4 fusion.15
  318.9 5.4 convolution_bitcast_fusion
  325.0 0.4 fusion.21
  325.4 0.4 fusion.22
  325.8 0.4 fusion.20
  326.2 0.4 fusion.13
  326.6 0.4 fusion.14
  327.0 0.4 fusion.1
  327.4 144.2 %all-reduce.11.cloned.1.call-done = f32[1024,256]{0,1:T(8,128)} async-done(((f32[1024,256]{0,1:T(8,128)}), f32[1024,256]{0,1:T(8,128)}) %all-reduce.11.cloned.1.call-update) | async-done | bytes 1048592 | tf_op jit(solution)/shard_map/psum | solution.py:42
  471.7 2.9 fusion.178
  475.0 65.0 %all-reduce.13.cloned.1.call-done = f32[256,256]{1,0:T(8,128)} async-done(((f32[256,256]{1,0:T(8,128)}), f32[256,256]{1,0:T(8,128)}) %all-reduce.13.cloned.1.call-update) | async-done | bytes 262160 | tf_op jit(solution)/shard_map/psum | solution.py:44
  540.0 1.3 fusion.179
  541.3 1.0 select_reduce_fusion
  543.0 0.4 fusion.25
  543.4 0.4 fusion.24
  543.9 0.4 fusion.23
  545.1 0.4 fusion.29
  546.3 0.4 fusion.11
  546.7 0.4 fusion.12
  547.2 0.4 fusion
  548.4 2.0 fusion.181
  (25 shorter events, 4.1 us)
Async XLA Ops:
  6.5 1.2 copy-start
  6.5 6.3 %copy-start.2 = (s32[4]{0:T(128)S(1)}, s32[4]{0:T(128)}, u32[]{:S(2)}) copy-start(s32[4]{0:T(128)} %param.6) | copy-start | bytes 52
  6.5 75.8 %all-reduce.7.cloned.1.call-start = ((), (), s32[]{:S(2)}) async-start(), calls=%async_computation | async-start | bytes 2097152 | tf_op jit(solution)/shard_map/psum | solution.py:36
  12.8 222.2 %all-reduce.9.cloned.1.call-start = ((), (), s32[]{:S(2)}) async-start(), calls=%async_computation.1 | async-start | bytes 2097152 | tf_op jit(solution)/shard_map/psum | solution.py:37
  87.8 224.2 %all-reduce.15.cloned.1.call-start = ((), (), s32[]{:S(2)}) async-start(), calls=%async_computation.4 | async-start | bytes 2621440 | tf_op jit(solution)/shard_map/psum | solution.py:39
  243.3 228.4 %all-reduce.11.cloned.1.call-start = ((), (), s32[]{:S(2)}) async-start(), calls=%async_computation.2 | async-start | bytes 2097152 | tf_op jit(solution)/shard_map/psum | solution.py:42
  324.3 215.7 %all-reduce.13.cloned.1.call-start = ((), (), s32[]{:S(2)}) async-start(), calls=%async_computation.3 | async-start | bytes 524288 | tf_op jit(solution)/shard_map/psum | solution.py:44
  543.8 4.5 copy-start.1
Sparse Core Ops, SparseCore 0:
  12.9 69.4 all-reduce.6
  87.9 147.0 all-reduce.8
  243.4 68.5 all-reduce.14
  324.5 147.1 all-reduce.10
  474.7 65.2 all-reduce.12

commit v2 on v1

v2 whole, which is shorter than its diff:
```python
import functools
import math

import jax
import jax.numpy as jnp
from jax import lax
from jax.experimental import pallas as pl
from jax.experimental.pallas import tpu as pltpu
from jax.sharding import PartitionSpec as P

D = 8192
NS_STEPS = 5
NX, NY, NZ = 4, 4, 8
MESH = pl.DeviceIdType.MESH
BF = jnp.bfloat16
F32 = jnp.float32


def rows(ref, start, size):
    if not isinstance(start, int):
        start = pl.multiple_of(start, 8)
    return ref.at[pl.ds(start, size), :]


class Link:
    def __init__(self, send, recv):
        self.send, self.recv, self.count, self.sent = send, recv, 0, []

    def copy(self, src, dst, device):
        copy = pltpu.make_async_remote_copy(
            src_ref=src,
            dst_ref=dst,
            send_sem=self.send.at[self.count],
            recv_sem=self.recv.at[self.count],
            device_id=device,
            device_id_type=MESH,
        )
        copy.start()
        self.count += 1
        self.sent.append(copy)
        return copy

    def drain(self):
        for copy in self.sent:
            copy.wait_send()
        self.sent = []


def take(copies):
    for copy in copies:
        copy.wait_recv()


def reduce_ring(link, work, into, base, at, n, size, right, left, slots):
    half, reach = size // 2, n // 2

    def shard(ref, index, offset, extent):
        return rows(ref, base + lax.rem(index + n, n) * size + offset, extent)

    def slot(way, step, offset, extent):
        return rows(slots, (way * reach + step) * size + offset, extent)

    ways = ((1, 0, right), (-1, half, left))
    coming = []
    for way, (sign, offset, device) in enumerate(ways):
        coming.append(
            [link.copy(shard(work, at + reach, offset, half), slot(way, 0, offset, half), device)]
        )
    ahead = []
    for way, (sign, offset, device) in enumerate(ways):
        ahead.append(
            link.copy(
                shard(work, at + sign * (reach - 1), half - offset, half),
                slot(way, 1, half - offset, half),
                device,
            )
        )
    for step in range(1, reach):
        yield
        for way, (sign, offset, device) in enumerate(ways):
            take(coming[way])
            skip, extent = (offset, half) if step == 1 else (0, size)
            target = shard(work, at + sign * (reach - step), skip, extent)
            target[...] = target[...] + slot(way, step - 1, skip, extent)[...]
            coming[way] = [link.copy(target, slot(way, step, skip, extent), device)]
            if step == 1:
                coming[way].append(ahead[way])
    yield
    take(coming[0])
    take(coming[1])
    shard(into, at, 0, size)[...] = (
        shard(work, at, 0, size)[...]
        + slot(0, reach - 1, 0, size)[...]
        + slot(1, reach - 1, 0, size)[...]
    )


def gather_ring(link, into, base, at, n, size, right, left, also=None):
    half, reach = size // 2, n // 2

    def shard(index, offset, extent):
        return rows(into, base + lax.rem(index + n, n) * size + offset, extent)

    def push(index, pieces, device):
        return [
            link.copy(shard(index, offset, extent), shard(index, offset, extent), device)
            for offset, extent in pieces
        ]

    ways = ((1, 0, right), (-1, half, left))
    whole, split = lambda offset: ((0, size),), lambda offset: ((offset, half), (half - offset, half))
    coming, late = [], []
    for sign, offset, device in ways:
        coming.append(push(at, (split if reach == 2 else whole)(offset), device))
    if also is not None:
        also(shard(at, 0, size))
    for step in range(1, reach):
        yield
        for way, (sign, offset, device) in enumerate(ways):
            origin = at - sign * step
            if step == reach - 1:
                take(coming[way][:1])
                late.append((origin, coming[way][1:], half - offset))
                if also is not None:
                    also(shard(origin, offset, half))
                coming[way] = push(origin, ((offset, half),), device)
            else:
                take(coming[way])
                pieces = split if step == reach - 2 else whole
                if also is not None:
                    also(shard(origin, 0, size))
                coming[way] = push(origin, pieces(offset), device)
    yield
    for origin, copies, offset in late:
        take(copies)
        if also is not None:
            also(shard(origin, offset, half))
    for way, (sign, offset, device) in enumerate(ways):
        take(coming[way])
        if also is not None:
            also(shard(at - sign * reach, offset, half))


def feat_total(link, place, work, into, near, slots, extent):
    half = extent // 2
    quarter = half // NX
    mine, other = place["core"] * half, (1 - place["core"]) * half
    pairs = []
    for offset in (2, 1, 3, 0):
        start = lax.rem(place["x"] + offset, NX) * quarter
        pairs.append(
            (
                start,
                link.copy(
                    rows(work, other + start, quarter), rows(near, start, quarter), place["partner"]
                ),
            )
        )
    yield
    for start, copy in pairs:
        copy.wait_recv()
        target = rows(work, mine + start, quarter)
        target[...] = target[...] + rows(near, start, quarter)[...]
    right, left = place["right_x"], place["left_x"]
    yield from reduce_ring(
        link, work, into, mine, place["x"], NX, quarter, right, left, slots
    )
    shared = []

    def also(ref):
        shared.append(link.copy(ref, ref, place["partner"]))

    yield from gather_ring(link, into, mine, place["x"], NX, quarter, right, left, also)
    yield
    take(shared)


def cohort_total(link, place, work, into, slots, base, extent, order):
    first, second = order
    n, m = place["size_" + first], place["size_" + second]
    size, small = extent // n, extent // n // m
    i, j = place[first], place[second]
    cut = n * size
    ring = (place["right_" + first], place["left_" + first])
    inner = (place["right_" + second], place["left_" + second])
    near = base + i * size
    yield from reduce_ring(link, work, work, base, i, n, size, *ring, rows(slots, 0, cut))
    yield from reduce_ring(
        link, work, into, near, j, m, small, *inner, rows(slots, cut, m * small)
    )
    yield from gather_ring(link, into, near, j, m, small, *inner)
    yield from gather_ring(link, into, base, i, n, size, *ring)


def run(*streams):
    streams = list(streams)
    while streams:
        for stream in list(streams):
            try:
                next(stream)
            except StopIteration:
                streams.remove(stream)


def halves(value):
    high = value.astype(BF)
    return high, (value - high.astype(F32)).astype(BF)


def dot(left, right, dims=(((1,), (0,)), ((), ()))):
    return lax.dot_general(left, right, dims, preferred_element_type=F32)


def product(left, right, dims=(((1,), (0,)), ((), ()))):
    (lh, ll), (rh, rl) = left, right
    return dot(lh, rh, dims) + (dot(lh, rl, dims) + dot(ll, rh, dims))


def times(left, right):
    return product(halves(left), halves(right))


def inverse_root(total):
    guess = lax.rsqrt(total)
    return guess * (1.5 - 0.5 * total * guess * guess)


def diagonal(p):
    return lax.broadcasted_iota(jnp.int32, (p, p), 0) == lax.broadcasted_iota(jnp.int32, (p, p), 1)


def root_of_trace(gram):
    total = jnp.sum(jnp.where(diagonal(gram.shape[0]), gram, 0.0), keepdims=True)
    return inverse_root(total)


def newton(gram, step, turn):
    p = gram.shape[0]
    for at in range(NS_STEPS):
        step[...] = jnp.where(diagonal(p), 1.5, 0.0) - 0.5 * gram[...]
        if at == 0:
            turn[...] = step[...]
        else:
            turn[...] = times(turn[...], step[...])
        if at + 1 < NS_STEPS:
            yield
            gram[...] = times(gram[...], step[...])
            yield
            gram[...] = times(gram[...], step[...])
            yield


def kernel(
    ranks, b_hbm, a_hbm, p_hbm, out,
    stage, a_high, a_low, b_high, b_low, y_high, y_low, c_high, c_low,
    work_a, into_a, near_a, slots_a,
    work_b, into_b, near_b, slots_b,
    work_g, into_g, near_g, slots_g,
    panel_one, panel_two, whole_one, whole_two, rings_one, rings_two,
    probe, gram, step, turn_one, turn_two,
    send, recv, local,
):
    clients, features, rank = b_hbm.shape
    p = probe.shape[1]
    slots = clients * rank
    cohort, feat = lax.axis_index("cohort"), lax.axis_index("feat")
    z, y = lax.div(cohort, NY), lax.rem(cohort, NY)
    x, core = lax.div(feat, 2), lax.rem(feat, 2)
    place = {
        "x": x, "y": y, "z": z, "core": core, "size_y": NY, "size_z": NZ,
        "partner": (cohort, x * 2 + 1 - core),
        "right_x": (cohort, lax.rem(x + 1, NX) * 2 + core),
        "left_x": (cohort, lax.rem(x + NX - 1, NX) * 2 + core),
        "right_y": (z * NY + lax.rem(y + 1, NY), feat),
        "left_y": (z * NY + lax.rem(y + NY - 1, NY), feat),
        "right_z": (lax.rem(z + 1, NZ) * NY + y, feat),
        "left_z": (lax.rem(z + NZ - 1, NZ) * NY + y, feat),
    }
    peers = [place[k] for k in ("partner", "right_x", "left_x", "right_y", "left_y", "right_z", "left_z")]

    load_p = pltpu.make_async_copy(p_hbm, probe, local.at[0])
    load_p.start()
    load_a = [
        pltpu.make_async_copy(a_hbm.at[c], stage.at[pl.ds(c * rank, rank), :], local.at[1 + c])
        for c in range(clients)
    ]
    for copy in load_a:
        copy.start()

    barrier = pltpu.get_barrier_semaphore()
    for peer in peers:
        pl.semaphore_signal(barrier, inc=1, device_id=peer, device_id_type=MESH)

    link = Link(send, recv)
    load_p.wait()
    y_high[...], y_low[...] = halves(probe[...])
    for c in range(clients):
        load_a[c].wait()
        at = pl.ds(c * rank, rank)
        a_high[at, :], a_low[at, :] = halves(stage[at, :])
    pl.semaphore_wait(barrier, len(peers))

    def client_coef(c):
        at = pl.ds(pl.multiple_of(c * rank, 8), rank)
        total = product((a_high[at, :], a_low[at, :]), (y_high[...], y_low[...]))
        live = lax.broadcasted_iota(jnp.int32, total.shape, 0) < ranks[c]
        return jnp.where(live, total, 0.0)

    def coef_half(work, which, half):
        def one(k, carry):
            start = which * half + k * rank
            work[pl.ds(pl.multiple_of(start, 8), rank), :] = client_coef(which * (clients // 2) + k)
            return carry
        lax.fori_loop(0, clients // 2, one, 0)

    coef_half(work_a, 1 - core, slots // 2)
    total = feat_total(link, place, work_a, into_a, near_a, slots_a, slots)
    next(total)
    coef_half(work_a, core, slots // 2)

    def b_stream():
        def fetch(c):
            return pltpu.make_async_copy(
                b_hbm.at[c], stage.at[:, pl.ds(c * rank, rank)], local.at[1 + clients + c]
            )
        loads = [fetch(c) for c in range(clients)]
        for copy in loads:
            copy.start()
        for c in range(clients):
            loads[c].wait()
            across = pl.ds(c * rank, rank)
            for k in range(2):
                at = pl.ds(k * (features // 2), features // 2)
                b_high[at, across], b_low[at, across] = halves(stage[at, across])
                yield

    run(total, b_stream())

    def panel_half(work, which):
        at = pl.ds(which * (features // 2), features // 2)
        work[at, :] = product((b_high[at, :], b_low[at, :]), (c_high[...], c_low[...]))

    def panel_total(work, into, rings, *others):
        half = features // 2
        panel_half(work, 0)
        upper = cohort_total(link, place, work, into, rows(rings, 0, 2 * half), 0, half, ("y", "z"))
        next(upper)
        panel_half(work, 1)
        lower = cohort_total(
            link, place, work, into, rows(rings, 2 * half, 2 * half), half, half, ("z", "y")
        )
        run(upper, lower, *others)

    c_high[...], c_low[...] = halves(into_a[...])
    panel_total(panel_one, whole_one, rings_one)
    link.drain()

    contract_rows = (((0,), (0,)), ((), ()))
    half_c, half_g = slots // 2, p // 2
    half = half_c + half_g
    y_high[...], y_low[...] = halves(whole_one[...])
    local_gram = product((y_high[...], y_low[...]), (y_high[...], y_low[...]), contract_rows)
    for which in range(2):
        work_b[pl.ds(which * half + half_c, half_g), :] = local_gram[which * half_g:(which + 1) * half_g]
    coef_half(work_b, 1 - core, half)
    total = feat_total(link, place, work_b, into_b, near_b, slots_b, slots + p)
    next(total)
    coef_half(work_b, core, half)
    run(total)

    for which in range(2):
        gram[pl.ds(which * half_g, half_g), :] = into_b[pl.ds(which * half + half_c, half_g), :]
    scale = root_of_trace(gram[...])
    gram[...] = gram[...] * (scale * scale)
    for which in range(2):
        at = pl.ds(which * half_c, half_c)
        c_high[at, :], c_low[at, :] = halves(into_b[pl.ds(which * half, half_c), :] * scale)
    panel_total(panel_two, whole_two, rings_two, newton(gram, step, turn_one))

    y_high[...], y_low[...] = halves(whole_two[...])
    work_g[...] = product((y_high[...], y_low[...]), (y_high[...], y_low[...]), contract_rows)
    run(feat_total(link, place, work_g, into_g, near_g, slots_g, p))
    gram[...] = times(times(turn_one[...], into_g[...]), turn_one[...])
    scale = root_of_trace(gram[...])
    gram[...] = gram[...] * (scale * scale)
    run(newton(gram, step, turn_two))
    last = times(turn_one[...], turn_two[...]) * (scale * math.sqrt(D))
    out[...] = product((y_high[...], y_low[...]), halves(last))
    link.drain()


def on_device(b_factors, a_factors, ranks, probes):
    clients, features, rank = b_factors.shape
    p = probes.shape[1]
    slots = clients * rank
    vm = pltpu.VMEM

    def feat_space(extent):
        return [
            vm((extent, p), F32), vm((extent, p), F32), vm((extent // 2, p), F32),
            vm((extent // 2, p), F32),
        ]

    scratch = (
        [vm((slots, features), F32)]
        + [vm((slots, features), BF)] * 2
        + [vm((features, slots), BF)] * 2
        + [vm((features, p), BF)] * 2
        + [vm((slots, p), BF)] * 2
        + feat_space(slots) + feat_space(slots + p) + feat_space(p)
        + [vm((features, p), F32)] * 4
        + [vm((2 * features, p), F32)] * 2
        + [vm((features, p), F32)]
        + [vm((p, p), F32)] * 4
        + [pltpu.SemaphoreType.DMA((200,)), pltpu.SemaphoreType.DMA((200,)), pltpu.SemaphoreType.DMA((1 + 2 * clients,))]
    )
    anywhere = pl.BlockSpec(memory_space=pl.ANY)
    return pl.pallas_call(
        kernel,
        out_shape=jax.ShapeDtypeStruct((features, p), F32),
        in_specs=[pl.BlockSpec(memory_space=pltpu.SMEM), anywhere, anywhere, anywhere],
        out_specs=pl.BlockSpec(memory_space=pltpu.VMEM),
        scratch_shapes=scratch,
        compiler_params=pltpu.CompilerParams(
            collective_id=0, has_side_effects=True, vmem_limit_bytes=60 << 20
        ),
    )(ranks, b_factors, a_factors, probes)


def solution(mesh):
    in_specs = (P("cohort", "feat", None), P("cohort", None, "feat"), P("cohort"), P("feat", None))
    out_specs = P("feat", None)
    return jax.shard_map(
        on_device, mesh=mesh, in_specs=in_specs, out_specs=out_specs, check_vma=False
    )
```

time: 558 us -> 173 us (0.31)
  waiting for transfers between devices: 495 us -> 0 us
  Pallas kernels: 0 us -> 169 us
  matrix products: 44.2 us -> 0 us
  between operations: 14.8 us -> 0.01 us
    psum x5 -> x0, waiting for transfers between devices: 495 us -> none  [the longest x1 147 us: on_device(): first = lax.psum(big('cdr,crp->dp', b_factors, coef), 'cohort')]
    pallas_call x0 -> x1, Pallas kernels: none -> 169 us  [on_device(): pl.pallas_call(kernel, out_shape=jax.ShapeDtypeStruct((features, p), F32)...]
    dot_general x34 -> x0, matrix products: 44.2 us -> none  [the longest x7 28.9 us: big(): jnp.einsum(spec, left, right, precision=lax.Precision.HIGH, preferred_ele...]
  transfers between devices with their start and end apart: 5 -> 0, of which waited for: 5 -> 0; matrix products, arithmetic and copies ran while one was open for 1% -> 0% of each run, Pallas kernels for 0% -> 0%
where the time goes in v2:
time: 173 us; the launch traced here: 171 us
  Pallas kernels  169 us (98%)
  local copies, waits for them, and re-layouts  2.26 us (1%)
    pallas_call x1, Pallas kernels, on_device(): pl.pallas_call(kernel, out_shape=jax.ShapeDtypeStruct((features, p), F32)...  169 us

profile of v2, /device:TPU:1, one launch (start us, length us, event | category | flops | bytes accessed | tf_op | source)
XLA Modules:
  0.0 171.1 jit_solution(11579021578377134498)
XLA Ops:
  0.0 168.8 %shard_map.46 = f32[1024,256]{1,0:T(8,128)} custom-call(s32[4]{0:T(128)} %ranks.1, f32[4,1024,256]{2,1,0:T(8,128)} %b_hbm.1, f32[4,256,1024]{2,1,0:T(8,128)} %a_hbm.1, f32[1024,256]{1,0:T(8,128)} %p_hbm.1), custom_call_target="tpu_custom_call" | custom-call | tf_op jit(solution)/shard_map/pallas_call | solution.py:418
  168.8 2.3 %copy.6 = f32[1024,256]{1,0:T(8,128)} copy(f32[1024,256]{1,0:T(8,128)} %shard_map.46) | data formatting | bytes 2097152

commit v3 on v2

--- a/solution.py
+++ b/solution.py
@@ -12,6 +12,7 @@
 NS_STEPS = 5
 NX, NY, NZ = 4, 4, 8
 MESH = pl.DeviceIdType.MESH
+FAR_FIRST = {4: (2, 1, 3), 8: (4, 3, 5, 2, 6, 1, 7)}
 BF = jnp.bfloat16
 F32 = jnp.float32
 
@@ -51,145 +52,148 @@
         copy.wait_recv()
 
 
-def reduce_ring(link, work, into, base, at, n, size, right, left, slots):
-    half, reach = size // 2, n // 2
-
-    def shard(ref, index, offset, extent):
-        return rows(ref, base + lax.rem(index + n, n) * size + offset, extent)
-
-    def slot(way, step, offset, extent):
-        return rows(slots, (way * reach + step) * size + offset, extent)
-
-    ways = ((1, 0, right), (-1, half, left))
+def reduce_direct(link, work, into, base, at, n, size, device, slots, ready=None):
     coming = []
-    for way, (sign, offset, device) in enumerate(ways):
+    for offset in FAR_FIRST[n]:
+        start = base + lax.rem(at + offset, n) * size
+        if ready is not None:
+            ready(offset)
         coming.append(
-            [link.copy(shard(work, at + reach, offset, half), slot(way, 0, offset, half), device)]
-        )
-    ahead = []
-    for way, (sign, offset, device) in enumerate(ways):
-        ahead.append(
             link.copy(
-                shard(work, at + sign * (reach - 1), half - offset, half),
-                slot(way, 1, half - offset, half),
-                device,
+                rows(work, start, size), rows(slots, (offset - 1) * size, size), device(offset)
             )
         )
-    for step in range(1, reach):
-        yield
-        for way, (sign, offset, device) in enumerate(ways):
-            take(coming[way])
-            skip, extent = (offset, half) if step == 1 else (0, size)
-            target = shard(work, at + sign * (reach - step), skip, extent)
-            target[...] = target[...] + slot(way, step - 1, skip, extent)[...]
-            coming[way] = [link.copy(target, slot(way, step, skip, extent), device)]
-            if step == 1:
-                coming[way].append(ahead[way])
-    yield
-    take(coming[0])
-    take(coming[1])
-    shard(into, at, 0, size)[...] = (
-        shard(work, at, 0, size)[...]
-        + slot(0, reach - 1, 0, size)[...]
-        + slot(1, reach - 1, 0, size)[...]
-    )
-
-
-def gather_ring(link, into, base, at, n, size, right, left, also=None):
-    half, reach = size // 2, n // 2
-
-    def shard(index, offset, extent):
-        return rows(into, base + lax.rem(index + n, n) * size + offset, extent)
-
-    def push(index, pieces, device):
-        return [
-            link.copy(shard(index, offset, extent), shard(index, offset, extent), device)
-            for offset, extent in pieces
+    if ready is not None:
+        ready(0)
+    yield
+    take(coming)
+    total = rows(work, base + at * size, size)[...]
+    for step in range(n - 1):
+        total = total + rows(slots, step * size, size)[...]
+    rows(into, base + at * size, size)[...] = total
+
+
+def gather_direct(link, into, base, at, n, size, device, also=None):
+    own = rows(into, base + at * size, size)
+    coming = [(offset, link.copy(own, own, device(offset))) for offset in FAR_FIRST[n]]
+    if also is not None:
+        also(own)
+    yield
+    for offset, copy in reversed(coming):
+        copy.wait_recv()
+        if also is not None:
+            also(rows(into, base + lax.rem(at + n - offset, n) * size, size))
+
+
+def reduce_pair_steps(link, work, into, base, at, n, size, device, slots):
+    half = size // 2
+
+    def shard(offset, skip, extent):
+        return rows(work, base + lax.rem(at + offset + n, n) * size + skip, extent)
+
+    def slot(index, extent):
+        return rows(slots, index * size, extent)
+
+    signs = ((1, 0, 0), (-1, half, 4))
+    coming, straight, joined = {}, [], []
+    for sign, skip, first in signs:
+        coming[sign] = [
+            link.copy(shard(4, skip, half), slot(first, half), device(2 * sign)),
+            link.copy(shard(3 * sign, 0, size), slot(first + 1, size), device(sign)),
         ]
-
-    ways = ((1, 0, right), (-1, half, left))
-    whole, split = lambda offset: ((0, size),), lambda offset: ((offset, half), (half - offset, half))
-    coming, late = [], []
-    for sign, offset, device in ways:
-        coming.append(push(at, (split if reach == 2 else whole)(offset), device))
-    if also is not None:
-        also(shard(at, 0, size))
-    for step in range(1, reach):
-        yield
-        for way, (sign, offset, device) in enumerate(ways):
-            origin = at - sign * step
-            if step == reach - 1:
-                take(coming[way][:1])
-                late.append((origin, coming[way][1:], half - offset))
-                if also is not None:
-                    also(shard(origin, offset, half))
-                coming[way] = push(origin, ((offset, half),), device)
-            else:
-                take(coming[way])
-                pieces = split if step == reach - 2 else whole
-                if also is not None:
-                    also(shard(origin, 0, size))
-                coming[way] = push(origin, pieces(offset), device)
-    yield
-    for origin, copies, offset in late:
-        take(copies)
-        if also is not None:
-            also(shard(origin, offset, half))
-    for way, (sign, offset, device) in enumerate(ways):
-        take(coming[way])
-        if also is not None:
-            also(shard(at - sign * reach, offset, half))
+    for sign, skip, first in signs:
+        straight.append(link.copy(shard(sign, 0, size), slot(first + 2, size), device(sign)))
+    yield
+    for sign, skip, first in signs:
+        take(coming[sign])
+        target = shard(2 * sign, 0, size)
+        target[...] = target[...] + slot(first + 1, size)[...]
+        part = shard(2 * sign, skip, half)
+        part[...] = part[...] + slot(first, half)[...]
+        joined.append(link.copy(target, slot(first + 3, size), device(2 * sign)))
+    yield
+    take(straight)
+    take(joined)
+    total = shard(0, 0, size)[...]
+    for index in (2, 3, 6, 7):
+        total = total + slot(index, size)[...]
+    rows(into, base + at * size, size)[...] = total
+
+
+def gather_pair_steps(link, into, base, at, n, size, device):
+    half = size // 2
+
+    def shard(offset, skip=0, extent=size):
+        return rows(into, base + lax.rem(at + offset + n, n) * size + skip, extent)
+
+    signs = ((1, 0), (-1, half))
+    far = {sign: link.copy(shard(0), shard(0), device(2 * sign)) for sign, skip in signs}
+    near = [link.copy(shard(0), shard(0), device(sign)) for sign, skip in signs]
+    yield
+    last = []
+    for sign, skip in signs:
+        far[sign].wait_recv()
+        passed = shard(-2 * sign, skip, half)
+        last.append(link.copy(passed, passed, device(2 * sign)))
+        passed = shard(-2 * sign)
+        last.append(link.copy(passed, passed, device(sign)))
+    yield
+    take(near)
+    take(last)
 
 
 def feat_total(link, place, work, into, near, slots, extent):
     half = extent // 2
     quarter = half // NX
-    mine, other = place["core"] * half, (1 - place["core"]) * half
-    pairs = []
-    for offset in (2, 1, 3, 0):
-        start = lax.rem(place["x"] + offset, NX) * quarter
-        pairs.append(
-            (
-                start,
-                link.copy(
-                    rows(work, other + start, quarter), rows(near, start, quarter), place["partner"]
-                ),
-            )
+    x, mine, other = place["x"], place["core"] * half, (1 - place["core"]) * half
+    pairs = {}
+    for offset in FAR_FIRST[NX] + (0,):
+        start = lax.rem(x + offset, NX) * quarter
+        pairs[offset] = (
+            start,
+            link.copy(rows(work, other + start, quarter), rows(near, start, quarter), place["partner"]),
         )
     yield
-    for start, copy in pairs:
+
+    def ready(offset):
+        start, copy = pairs[offset]
         copy.wait_recv()
         target = rows(work, mine + start, quarter)
         target[...] = target[...] + rows(near, start, quarter)[...]
-    right, left = place["right_x"], place["left_x"]
-    yield from reduce_ring(
-        link, work, into, mine, place["x"], NX, quarter, right, left, slots
+
+    yield from reduce_direct(
+        link, work, into, mine, x, NX, quarter, place["along_x"], slots, ready
     )
     shared = []
 
     def also(ref):
         shared.append(link.copy(ref, ref, place["partner"]))
 
-    yield from gather_ring(link, into, mine, place["x"], NX, quarter, right, left, also)
+    yield from gather_direct(link, into, mine, x, NX, quarter, place["along_x"], also)
     yield
     take(shared)
 
 
-def cohort_total(link, place, work, into, slots, base, extent, order):
-    first, second = order
-    n, m = place["size_" + first], place["size_" + second]
-    size, small = extent // n, extent // n // m
-    i, j = place[first], place[second]
-    cut = n * size
-    ring = (place["right_" + first], place["left_" + first])
-    inner = (place["right_" + second], place["left_" + second])
-    near = base + i * size
-    yield from reduce_ring(link, work, work, base, i, n, size, *ring, rows(slots, 0, cut))
-    yield from reduce_ring(
-        link, work, into, near, j, m, small, *inner, rows(slots, cut, m * small)
-    )
-    yield from gather_ring(link, into, near, j, m, small, *inner)
-    yield from gather_ring(link, into, base, i, n, size, *ring)
+def upper_total(link, place, work, into, slots, base, extent):
+    y, z = place["y"], place["z"]
+    size, small = extent // NY, extent // NY // NZ
+    near = base + y * size
+    along_y, along_z = place["along_y"], place["along_z"]
+    yield from reduce_direct(link, work, work, base, y, NY, size, along_y, rows(slots, 0, extent))
+    yield from reduce_direct(link, work, into, near, z, NZ, small, along_z, rows(slots, extent, size))
+    yield from gather_direct(link, into, near, z, NZ, small, along_z)
+    yield from gather_direct(link, into, base, y, NY, size, along_y)
+
+
+def lower_total(link, place, work, into, slots, base, extent):
+    y, z = place["y"], place["z"]
+    size, small = extent // NZ, extent // NZ // NY
+    near = base + z * size
+    along_y, along_z = place["along_y"], place["along_z"]
+    yield from reduce_pair_steps(link, work, work, base, z, NZ, size, along_z, rows(slots, 0, extent))
+    yield from reduce_direct(link, work, into, near, y, NY, small, along_y, rows(slots, extent, size))
+    yield from gather_direct(link, into, near, y, NY, small, along_y)
+    yield from gather_pair_steps(link, into, base, z, NZ, size, along_z)
 
 
 def run(*streams):
@@ -267,16 +271,15 @@
     z, y = lax.div(cohort, NY), lax.rem(cohort, NY)
     x, core = lax.div(feat, 2), lax.rem(feat, 2)
     place = {
-        "x": x, "y": y, "z": z, "core": core, "size_y": NY, "size_z": NZ,
+        "x": x, "y": y, "z": z, "core": core,
         "partner": (cohort, x * 2 + 1 - core),
-        "right_x": (cohort, lax.rem(x + 1, NX) * 2 + core),
-        "left_x": (cohort, lax.rem(x + NX - 1, NX) * 2 + core),
-        "right_y": (z * NY + lax.rem(y + 1, NY), feat),
-        "left_y": (z * NY + lax.rem(y + NY - 1, NY), feat),
-        "right_z": (lax.rem(z + 1, NZ) * NY + y, feat),
-        "left_z": (lax.rem(z + NZ - 1, NZ) * NY + y, feat),
+        "along_x": lambda d: (cohort, lax.rem(x + d + NX, NX) * 2 + core),
+        "along_y": lambda d: (z * NY + lax.rem(y + d + NY, NY), feat),
+        "along_z": lambda d: (lax.rem(z + d + NZ, NZ) * NY + y, feat),
     }
-    peers = [place[k] for k in ("partner", "right_x", "left_x", "right_y", "left_y", "right_z", "left_z")]
+    peers = [place["partner"]]
+    for axis, n in (("along_x", NX), ("along_y", NY), ("along_z", NZ)):
+        peers += [place[axis](d) for d in range(1, n)]
 
     load_p = pltpu.make_async_copy(p_hbm, probe, local.at[0])
     load_p.start()
@@ -342,14 +345,19 @@
 
     def panel_total(work, into, rings, *others):
         half = features // 2
+        panel_half(work, 1)
+        lower = lower_total(link, place, work, into, rows(rings, 2 * half, 2 * half), half, half)
+        next(lower)
         panel_half(work, 0)
-        upper = cohort_total(link, place, work, into, rows(rings, 0, 2 * half), 0, half, ("y", "z"))
+        upper = upper_total(link, place, work, into, rows(rings, 0, 2 * half), 0, half)
         next(upper)
-        panel_half(work, 1)
-        lower = cohort_total(
-            link, place, work, into, rows(rings, 2 * half, 2 * half), half, half, ("z", "y")
-        )
-        run(upper, lower, *others)
+        for stream in (lower, upper, lower, upper, lower, lower, upper, lower, upper, lower):
+            for other in others:
+                next(other, None)
+                next(other, None)
+            next(stream, None)
+        for other in others:
+            run(other)
 
     c_high[...], c_low[...] = halves(into_a[...])
     panel_total(panel_one, whole_one, rings_one)

time: 173 us -> 139 us (0.80)
  Pallas kernels: 169 us -> 137 us
    pallas_call x1, Pallas kernels: 169 us -> 137 us  [on_device(): pl.pallas_call(kernel, out_shape=jax.ShapeDtypeStruct((features, p), F32)...]
where the time goes in v3:
time: 139 us
  Pallas kernels  137 us (99%)
  local copies, waits for them, and re-layouts  2.26 us (2%)
    pallas_call x1, Pallas kernels, on_device(): pl.pallas_call(kernel, out_shape=jax.ShapeDtypeStruct((features, p), F32)...  137 us

profile of v3, /device:TPU:1, one launch (start us, length us, event | category | flops | bytes accessed | tf_op | source)
XLA Modules:
  0.0 138.8 jit_solution(5171284414963683720)
XLA Ops:
  0.0 136.5 %shard_map.46 = f32[1024,256]{1,0:T(8,128)} custom-call(s32[4]{0:T(128)} %ranks.1, f32[4,1024,256]{2,1,0:T(8,128)} %b_hbm.1, f32[4,256,1024]{2,1,0:T(8,128)} %a_hbm.1, f32[1024,256]{1,0:T(8,128)} %p_hbm.1), custom_call_target="tpu_custom_call" | custom-call | tf_op jit(solution)/shard_map/pallas_call | solution.py:426
  136.5 2.3 %copy.6 = f32[1024,256]{1,0:T(8,128)} copy(f32[1024,256]{1,0:T(8,128)} %shard_map.46) | data formatting | bytes 2097152

commit v4 on v3

--- a/solution.py
+++ b/solution.py
@@ -256,10 +256,11 @@
 
 def kernel(
     ranks, b_hbm, a_hbm, p_hbm, out,
-    stage, a_high, a_low, b_high, b_low, y_high, y_low, c_high, c_low,
+    stage, b_stage, a_high, a_low, b_high, b_low, y_high, y_low, c_high, c_low,
     work_a, into_a, near_a, slots_a,
     work_b, into_b, near_b, slots_b,
     work_g, into_g, near_g, slots_g,
+    work_h, into_h, near_h, slots_h,
     panel_one, panel_two, whole_one, whole_two, rings_one, rings_two,
     probe, gram, step, turn_one, turn_two,
     send, recv, local,
@@ -281,12 +282,18 @@
     for axis, n in (("along_x", NX), ("along_y", NY), ("along_z", NZ)):
         peers += [place[axis](d) for d in range(1, n)]
 
+    def load(source, into, c, sem):
+        start = pl.multiple_of(c * rank, rank)
+        across = into is b_stage
+        target = into.at[:, pl.ds(start, rank)] if across else into.at[pl.ds(start, rank), :]
+        return pltpu.make_async_copy(source.at[c], target, local.at[sem])
+
+    core, pairs = place["core"], clients // 2
+    wanted = [2 * k + 1 - core for k in range(pairs)] + [2 * k + core for k in range(pairs)]
     load_p = pltpu.make_async_copy(p_hbm, probe, local.at[0])
     load_p.start()
-    load_a = [
-        pltpu.make_async_copy(a_hbm.at[c], stage.at[pl.ds(c * rank, rank), :], local.at[1 + c])
-        for c in range(clients)
-    ]
+    load_a = [load(a_hbm, stage, c, 1 + k) for k, c in enumerate(wanted)]
+    load_b = [load(b_hbm, b_stage, c, 1 + clients + c) for c in range(clients)]
     for copy in load_a:
         copy.start()
 
@@ -297,98 +304,97 @@
     link = Link(send, recv)
     load_p.wait()
     y_high[...], y_low[...] = halves(probe[...])
-    for c in range(clients):
-        load_a[c].wait()
-        at = pl.ds(c * rank, rank)
-        a_high[at, :], a_low[at, :] = halves(stage[at, :])
-    pl.semaphore_wait(barrier, len(peers))
-
-    def client_coef(c):
-        at = pl.ds(pl.multiple_of(c * rank, 8), rank)
+
+    def client_coef(work, c):
+        at = pl.ds(pl.multiple_of(c * rank, rank), rank)
         total = product((a_high[at, :], a_low[at, :]), (y_high[...], y_low[...]))
         live = lax.broadcasted_iota(jnp.int32, total.shape, 0) < ranks[c]
-        return jnp.where(live, total, 0.0)
-
-    def coef_half(work, which, half):
-        def one(k, carry):
-            start = which * half + k * rank
-            work[pl.ds(pl.multiple_of(start, 8), rank), :] = client_coef(which * (clients // 2) + k)
-            return carry
-        lax.fori_loop(0, clients // 2, one, 0)
-
-    coef_half(work_a, 1 - core, slots // 2)
-    total = feat_total(link, place, work_a, into_a, near_a, slots_a, slots)
-    next(total)
-    coef_half(work_a, core, slots // 2)
+        work[at, :] = jnp.where(live, total, 0.0)
+
+    def feat_stream(spaces, k, extent):
+        work, into, near, slot_rows = spaces
+        return feat_total(
+            link, place, rows(work, k * extent, extent), rows(into, k * extent, extent),
+            rows(near, k * extent // 2, extent // 2), rows(slot_rows, k * extent // 2, extent // 2),
+            extent,
+        )
+
+    def coef_total(spaces, fetch, *others):
+        streams = [feat_stream(spaces, k, 2 * rank) for k in range(pairs)]
+        for k, c in enumerate(wanted):
+            fetch(k, c)
+            client_coef(spaces[0], c)
+            if k < pairs:
+                if k == 0 and fetch is first_fetch:
+                    pl.semaphore_wait(barrier, len(peers))
+                next(streams[k])
+        run(*streams, *others)
+
+    def first_fetch(k, c):
+        load_a[k].wait()
+        at = pl.ds(pl.multiple_of(c * rank, rank), rank)
+        a_high[at, :], a_low[at, :] = halves(stage[at, :])
+        if k == pairs - 1:
+            for copy in load_b:
+                copy.start()
 
     def b_stream():
-        def fetch(c):
-            return pltpu.make_async_copy(
-                b_hbm.at[c], stage.at[:, pl.ds(c * rank, rank)], local.at[1 + clients + c]
-            )
-        loads = [fetch(c) for c in range(clients)]
-        for copy in loads:
-            copy.start()
         for c in range(clients):
-            loads[c].wait()
+            load_b[c].wait()
             across = pl.ds(c * rank, rank)
             for k in range(2):
                 at = pl.ds(k * (features // 2), features // 2)
-                b_high[at, across], b_low[at, across] = halves(stage[at, across])
-                yield
-
-    run(total, b_stream())
-
-    def panel_half(work, which):
-        at = pl.ds(which * (features // 2), features // 2)
-        work[at, :] = product((b_high[at, :], b_low[at, :]), (c_high[...], c_low[...]))
+                b_high[at, across], b_low[at, across] = halves(b_stage[at, across])
+            yield
 
     def panel_total(work, into, rings, *others):
-        half = features // 2
-        panel_half(work, 1)
-        lower = lower_total(link, place, work, into, rows(rings, 2 * half, 2 * half), half, half)
-        next(lower)
-        panel_half(work, 0)
-        upper = upper_total(link, place, work, into, rows(rings, 0, 2 * half), 0, half)
-        next(upper)
-        for stream in (lower, upper, lower, upper, lower, lower, upper, lower, upper, lower):
-            for other in others:
-                next(other, None)
-                next(other, None)
-            next(stream, None)
-        for other in others:
-            run(other)
-
+        part = features // 4
+        streams = []
+        for k, kind in enumerate((lower_total, lower_total, upper_total, upper_total)):
+            at = pl.ds(k * part, part)
+            work[at, :] = product((b_high[at, :], b_low[at, :]), (c_high[...], c_low[...]))
+            streams.append(
+                kind(link, place, work, into, rows(rings, 2 * k * part, 2 * part), k * part, part)
+            )
+            next(streams[k])
+        for kind in (0, 1, 0, 1, 0, 0, 1, 0, 1, 0):
+            for stream in streams[2 * kind:2 * kind + 2]:
+                for other in others:
+                    next(other, None)
+                next(stream, None)
+        run(*others)
+
+    spaces_a = (work_a, into_a, near_a, slots_a)
+    spaces_b = (work_b, into_b, near_b, slots_b)
+    spaces_g = (work_g, into_g, near_g, slots_g)
+    spaces_h = (work_h, into_h, near_h, slots_h)
+    contract_rows = (((0,), (0,)), ((), ()))
+
+    def local_gram(work):
+        work[...] = product(
+            (y_high[...], y_low[...]), (y_high[...], y_low[...]), contract_rows
+        )
+
+    def gram_total(spaces):
+        local_gram(spaces[0])
+        yield from feat_stream(spaces, 0, p)
+
+    coef_total(spaces_a, first_fetch, b_stream())
     c_high[...], c_low[...] = halves(into_a[...])
     panel_total(panel_one, whole_one, rings_one)
     link.drain()
 
-    contract_rows = (((0,), (0,)), ((), ()))
-    half_c, half_g = slots // 2, p // 2
-    half = half_c + half_g
     y_high[...], y_low[...] = halves(whole_one[...])
-    local_gram = product((y_high[...], y_low[...]), (y_high[...], y_low[...]), contract_rows)
-    for which in range(2):
-        work_b[pl.ds(which * half + half_c, half_g), :] = local_gram[which * half_g:(which + 1) * half_g]
-    coef_half(work_b, 1 - core, half)
-    total = feat_total(link, place, work_b, into_b, near_b, slots_b, slots + p)
-    next(total)
-    coef_half(work_b, core, half)
-    run(total)
-
-    for which in range(2):
-        gram[pl.ds(which * half_g, half_g), :] = into_b[pl.ds(which * half + half_c, half_g), :]
+    coef_total(spaces_b, lambda k, c: None, gram_total(spaces_g))
+    gram[...] = into_g[...]
     scale = root_of_trace(gram[...])
     gram[...] = gram[...] * (scale * scale)
-    for which in range(2):
-        at = pl.ds(which * half_c, half_c)
-        c_high[at, :], c_low[at, :] = halves(into_b[pl.ds(which * half, half_c), :] * scale)
+    c_high[...], c_low[...] = halves(into_b[...] * scale)
     panel_total(panel_two, whole_two, rings_two, newton(gram, step, turn_one))
 
     y_high[...], y_low[...] = halves(whole_two[...])
-    work_g[...] = product((y_high[...], y_low[...]), (y_high[...], y_low[...]), contract_rows)
-    run(feat_total(link, place, work_g, into_g, near_g, slots_g, p))
-    gram[...] = times(times(turn_one[...], into_g[...]), turn_one[...])
+    run(gram_total(spaces_h))
+    gram[...] = times(times(turn_one[...], into_h[...]), turn_one[...])
     scale = root_of_trace(gram[...])
     gram[...] = gram[...] * (scale * scale)
     run(newton(gram, step, turn_two))
@@ -410,17 +416,17 @@
         ]
 
     scratch = (
-        [vm((slots, features), F32)]
+        [vm((slots, features), F32), vm((features, slots), F32)]
         + [vm((slots, features), BF)] * 2
         + [vm((features, slots), BF)] * 2
         + [vm((features, p), BF)] * 2
         + [vm((slots, p), BF)] * 2
-        + feat_space(slots) + feat_space(slots + p) + feat_space(p)
+        + feat_space(slots) * 2 + feat_space(p) * 2
         + [vm((features, p), F32)] * 4
         + [vm((2 * features, p), F32)] * 2
         + [vm((features, p), F32)]
         + [vm((p, p), F32)] * 4
-        + [pltpu.SemaphoreType.DMA((200,)), pltpu.SemaphoreType.DMA((200,)), pltpu.SemaphoreType.DMA((1 + 2 * clients,))]
+        + [pltpu.SemaphoreType.DMA((260,)), pltpu.SemaphoreType.DMA((260,)), pltpu.SemaphoreType.DMA((1 + 2 * clients,))]
     )
     anywhere = pl.BlockSpec(memory_space=pl.ANY)
     return pl.pallas_call(

time: 139 us -> 131 us (0.942)
  Pallas kernels: 137 us -> 128 us
    pallas_call x1, Pallas kernels: 137 us -> 128 us  [on_device(): pl.pallas_call(kernel, out_shape=jax.ShapeDtypeStruct((features, p), F32)...]
where the time goes in v4:
time: 131 us
  Pallas kernels  128 us (98%)
  local copies, waits for them, and re-layouts  2.26 us (2%)
    pallas_call x1, Pallas kernels, on_device(): pl.pallas_call(kernel, out_shape=jax.ShapeDtypeStruct((features, p), F32)...  128 us

profile of v4, /device:TPU:1, one launch (start us, length us, event | category | flops | bytes accessed | tf_op | source)
XLA Modules:
  0.0 130.7 jit_solution(6189628801125228364)
XLA Ops:
  0.0 128.4 %shard_map.46 = f32[1024,256]{1,0:T(8,128)} custom-call(s32[4]{0:T(128)} %ranks.1, f32[4,1024,256]{2,1,0:T(8,128)} %b_hbm.1, f32[4,256,1024]{2,1,0:T(8,128)} %a_hbm.1, f32[1024,256]{1,0:T(8,128)} %p_hbm.1), custom_call_target="tpu_custom_call" | custom-call | tf_op jit(solution)/shard_map/pallas_call | solution.py:432
  128.4 2.3 %copy.6 = f32[1024,256]{1,0:T(8,128)} copy(f32[1024,256]{1,0:T(8,128)} %shard_map.46) | data formatting | bytes 2097152

commit v5 on v4

--- a/solution.py
+++ b/solution.py
@@ -259,8 +259,7 @@
     stage, b_stage, a_high, a_low, b_high, b_low, y_high, y_low, c_high, c_low,
     work_a, into_a, near_a, slots_a,
     work_b, into_b, near_b, slots_b,
-    work_g, into_g, near_g, slots_g,
-    work_h, into_h, near_h, slots_h,
+    work_g, into_g, slots_g, work_h, into_h, slots_h, marks,
     panel_one, panel_two, whole_one, whole_two, rings_one, rings_two,
     probe, gram, step, turn_one, turn_two,
     send, recv, local,
@@ -274,12 +273,14 @@
     place = {
         "x": x, "y": y, "z": z, "core": core,
         "partner": (cohort, x * 2 + 1 - core),
+        "feat": feat,
+        "along_feat": lambda d: (cohort, lax.rem(feat + d, 2 * NX)),
         "along_x": lambda d: (cohort, lax.rem(x + d + NX, NX) * 2 + core),
         "along_y": lambda d: (z * NY + lax.rem(y + d + NY, NY), feat),
         "along_z": lambda d: (lax.rem(z + d + NZ, NZ) * NY + y, feat),
     }
-    peers = [place["partner"]]
-    for axis, n in (("along_x", NX), ("along_y", NY), ("along_z", NZ)):
+    peers = []
+    for axis, n in (("along_feat", 2 * NX), ("along_y", NY), ("along_z", NZ)):
         peers += [place[axis](d) for d in range(1, n)]
 
     def load(source, into, c, sem):
@@ -305,11 +306,15 @@
     load_p.wait()
     y_high[...], y_low[...] = halves(probe[...])
 
-    def client_coef(work, c):
-        at = pl.ds(pl.multiple_of(c * rank, rank), rank)
-        total = product((a_high[at, :], a_low[at, :]), (y_high[...], y_low[...]))
-        live = lax.broadcasted_iota(jnp.int32, total.shape, 0) < ranks[c]
-        work[at, :] = jnp.where(live, total, 0.0)
+    def client_coef(work, c, start, extent, begin, end):
+        at, part = pl.ds(pl.multiple_of(c * rank, rank), rank), pl.ds(start, extent)
+        total = product((a_high[at, part], a_low[at, part]), (y_high[part, :], y_low[part, :]))
+        if not begin:
+            total = total + work[at, :]
+        if end:
+            live = lax.broadcasted_iota(jnp.int32, total.shape, 0) < ranks[c]
+            total = jnp.where(live, total, 0.0)
+        work[at, :] = total
 
     def feat_stream(spaces, k, extent):
         work, into, near, slot_rows = spaces
@@ -319,24 +324,24 @@
             extent,
         )
 
-    def coef_total(spaces, fetch, *others):
+    def coef_total(spaces, coef, *others):
         streams = [feat_stream(spaces, k, 2 * rank) for k in range(pairs)]
         for k, c in enumerate(wanted):
-            fetch(k, c)
-            client_coef(spaces[0], c)
+            coef(k, c)
             if k < pairs:
-                if k == 0 and fetch is first_fetch:
-                    pl.semaphore_wait(barrier, len(peers))
                 next(streams[k])
         run(*streams, *others)
 
-    def first_fetch(k, c):
+    def first_coef(k, c):
         load_a[k].wait()
         at = pl.ds(pl.multiple_of(c * rank, rank), rank)
         a_high[at, :], a_low[at, :] = halves(stage[at, :])
         if k == pairs - 1:
             for copy in load_b:
                 copy.start()
+        client_coef(work_a, c, 0, features, True, True)
+        if k == 0:
+            pl.semaphore_wait(barrier, len(peers))
 
     def b_stream():
         for c in range(clients):
@@ -347,9 +352,10 @@
                 b_high[at, across], b_low[at, across] = halves(b_stage[at, across])
             yield
 
-    def panel_total(work, into, rings, *others):
-        part = features // 4
-        streams = []
+    part = features // 4
+
+    def panel_total(work, into, rings, done, *others):
+        streams, open_streams = [], set(range(4))
         for k, kind in enumerate((lower_total, lower_total, upper_total, upper_total)):
             at = pl.ds(k * part, part)
             work[at, :] = product((b_high[at, :], b_low[at, :]), (c_high[...], c_low[...]))
@@ -358,42 +364,75 @@
             )
             next(streams[k])
         for kind in (0, 1, 0, 1, 0, 0, 1, 0, 1, 0):
-            for stream in streams[2 * kind:2 * kind + 2]:
+            for k in (2 * kind, 2 * kind + 1):
                 for other in others:
                     next(other, None)
-                next(stream, None)
+                if k in open_streams and next(streams[k], part) == part:
+                    open_streams.remove(k)
+                    done(k, len(open_streams))
         run(*others)
 
     spaces_a = (work_a, into_a, near_a, slots_a)
     spaces_b = (work_b, into_b, near_b, slots_b)
-    spaces_g = (work_g, into_g, near_g, slots_g)
-    spaces_h = (work_h, into_h, near_h, slots_h)
     contract_rows = (((0,), (0,)), ((), ()))
 
-    def local_gram(work):
-        work[...] = product(
-            (y_high[...], y_low[...]), (y_high[...], y_low[...]), contract_rows
-        )
-
-    def gram_total(spaces):
-        local_gram(spaces[0])
-        yield from feat_stream(spaces, 0, p)
-
-    coef_total(spaces_a, first_fetch, b_stream())
+    def split_rows(whole, k):
+        at = pl.ds(k * part, part)
+        y_high[at, :], y_low[at, :] = halves(whole[at, :])
+        return at
+
+    def add_gram(work, at, begin):
+        value = (y_high[at, :], y_low[at, :])
+        total = product(value, value, contract_rows)
+        work[...] = total if begin else work[...] + total
+
+    def gram_total(work, into, slot_rows):
+        each = p // (2 * NX)
+        ring = (place["feat"], 2 * NX, each, place["along_feat"])
+        yield from reduce_direct(link, work, into, 0, *ring, slot_rows)
+        yield from gather_direct(link, into, 0, *ring)
+
+    def trace_total():
+        square = whole_one[...] * whole_one[...]
+        own = pl.ds(pl.multiple_of(place["feat"] * 8, 8), 8)
+        marks[own, :] = jnp.sum(square.reshape(features // 8, 8, p), axis=0)
+        yield from gather_direct(link, marks, 0, place["feat"], 2 * NX, 8, place["along_feat"])
+
+    coef_total(spaces_a, first_coef, b_stream())
     c_high[...], c_low[...] = halves(into_a[...])
-    panel_total(panel_one, whole_one, rings_one)
+
+    last_part = []
+
+    def first_done(k, left):
+        at = split_rows(whole_one, k)
+        if left:
+            for c in range(clients):
+                client_coef(work_b, c, k * part, part, left == 3, False)
+        else:
+            last_part.append(k * part)
+
+    panel_total(panel_one, whole_one, rings_one, first_done)
     link.drain()
 
-    y_high[...], y_low[...] = halves(whole_one[...])
-    coef_total(spaces_b, lambda k, c: None, gram_total(spaces_g))
-    gram[...] = into_g[...]
-    scale = root_of_trace(gram[...])
-    gram[...] = gram[...] * (scale * scale)
-    c_high[...], c_low[...] = halves(into_b[...] * scale)
-    panel_total(panel_two, whole_two, rings_two, newton(gram, step, turn_one))
-
-    y_high[...], y_low[...] = halves(whole_two[...])
-    run(gram_total(spaces_h))
+    coef_total(
+        spaces_b, lambda k, c: client_coef(work_b, c, last_part[0], part, False, True), trace_total()
+    )
+    scale_one = inverse_root(jnp.sum(marks[...], keepdims=True))
+    c_high[...], c_low[...] = halves(into_b[...] * scale_one)
+
+    def first_turn():
+        for k in range(4):
+            add_gram(work_g, pl.ds(k * part, part), k == 0)
+        yield from gram_total(work_g, into_g, slots_g)
+        gram[...] = into_g[...] * (scale_one * scale_one)
+        yield from newton(gram, step, turn_one)
+
+    def second_done(k, left):
+        add_gram(work_h, split_rows(whole_two, k), left == 3)
+
+    panel_total(panel_two, whole_two, rings_two, second_done, first_turn())
+
+    run(gram_total(work_h, into_h, slots_h))
     gram[...] = times(times(turn_one[...], into_h[...]), turn_one[...])
     scale = root_of_trace(gram[...])
     gram[...] = gram[...] * (scale * scale)
@@ -421,14 +460,14 @@
         + [vm((features, slots), BF)] * 2
         + [vm((features, p), BF)] * 2
         + [vm((slots, p), BF)] * 2
-        + feat_space(slots) * 2 + feat_space(p) * 2
+        + feat_space(slots) * 2 + [vm((p, p), F32)] * 6 + [vm((16 * NX, p), F32)]
         + [vm((features, p), F32)] * 4
         + [vm((2 * features, p), F32)] * 2
         + [vm((features, p), F32)]
         + [vm((p, p), F32)] * 4
-        + [pltpu.SemaphoreType.DMA((260,)), pltpu.SemaphoreType.DMA((260,)), pltpu.SemaphoreType.DMA((1 + 2 * clients,))]
+        + [pltpu.SemaphoreType.DMA((280,)), pltpu.SemaphoreType.DMA((280,)), pltpu.SemaphoreType.DMA((1 + 2 * clients,))]
     )
-    anywhere = pl.BlockSpec(memory_space=pl.ANY)
+    anywhere = pl.BlockSpec(memory_space=pltpu.MemorySpace.HBM)
     return pl.pallas_call(
         kernel,
         out_shape=jax.ShapeDtypeStruct((features, p), F32),
@@ -436,7 +475,7 @@
         out_specs=pl.BlockSpec(memory_space=pltpu.VMEM),
         scratch_shapes=scratch,
         compiler_params=pltpu.CompilerParams(
-            collective_id=0, has_side_effects=True, vmem_limit_bytes=60 << 20
+            collective_id=0, has_side_effects=True, vmem_limit_bytes=52 << 20
         ),
     )(ranks, b_factors, a_factors, probes)
 

time: 131 us -> 128 us (0.977)
  Pallas kernels: 128 us -> 126 us
    pallas_call x1, Pallas kernels: 128 us -> 126 us  [on_device(): pl.pallas_call(kernel, out_shape=jax.ShapeDtypeStruct((features, p), F32)...]
where the time goes in v5:
time: 128 us
  Pallas kernels  126 us (98%)
  local copies, waits for them, and re-layouts  1.63 us (1%)
    pallas_call x1, Pallas kernels, on_device(): pl.pallas_call(kernel, out_shape=jax.ShapeDtypeStruct((features, p), F32)...  126 us

profile of v5, /device:TPU:1, one launch (start us, length us, event | category | flops | bytes accessed | tf_op | source)
XLA Modules:
  0.0 127.8 jit_solution(15871273065058037318)
XLA Ops:
  0.0 0.0 copy-start
  0.0 0.7 copy-done
  0.7 126.2 %shard_map.46 = f32[1024,256]{1,0:T(8,128)S(1)} custom-call(s32[4]{0:T(128)S(1)} %copy-done, f32[4,1024,256]{2,1,0:T(8,128)} %b_hbm.1, f32[4,256,1024]{2,1,0:T(8,128)} %a_hbm.1, f32[1024,256]{1,0:T(8,128)} %p_hbm.1), custom_call_target="tpu_custom_call" | custom-call | tf_op jit(solution)/shard_map/pallas_call | solution.py:471
  126.8 1.0 copy.6
Async XLA Ops:
  0.0 0.7 copy-start

commit v6 on v5

--- a/solution.py
+++ b/solution.py
@@ -238,19 +238,15 @@
     return inverse_root(total)
 
 
-def newton(gram, step, turn):
-    p = gram.shape[0]
+def newton(gram, turn):
     for at in range(NS_STEPS):
-        step[...] = jnp.where(diagonal(p), 1.5, 0.0) - 0.5 * gram[...]
-        if at == 0:
-            turn[...] = step[...]
-        else:
-            turn[...] = times(turn[...], step[...])
+        step = jnp.where(diagonal(gram.shape[0]), 1.5, 0.0) - 0.5 * gram[...]
+        split = halves(step)
+        turn[...] = step if at == 0 else product(halves(turn[...]), split)
         if at + 1 < NS_STEPS:
-            yield
-            gram[...] = times(gram[...], step[...])
-            yield
-            gram[...] = times(gram[...], step[...])
+            for factor in range(2):
+                yield
+                gram[...] = product(halves(gram[...]), split)
             yield
 
 
@@ -261,7 +257,7 @@
     work_b, into_b, near_b, slots_b,
     work_g, into_g, slots_g, work_h, into_h, slots_h, marks,
     panel_one, panel_two, whole_one, whole_two, rings_one, rings_two,
-    probe, gram, step, turn_one, turn_two,
+    probe, gram, turn_one, turn_two,
     send, recv, local,
 ):
     clients, features, rank = b_hbm.shape
@@ -283,6 +279,10 @@
     for axis, n in (("along_feat", 2 * NX), ("along_y", NY), ("along_z", NZ)):
         peers += [place[axis](d) for d in range(1, n)]
 
+    barrier = pltpu.get_barrier_semaphore()
+    for peer in peers:
+        pl.semaphore_signal(barrier, inc=1, device_id=peer, device_id_type=MESH)
+
     def load(source, into, c, sem):
         start = pl.multiple_of(c * rank, rank)
         across = into is b_stage
@@ -297,10 +297,6 @@
     load_b = [load(b_hbm, b_stage, c, 1 + clients + c) for c in range(clients)]
     for copy in load_a:
         copy.start()
-
-    barrier = pltpu.get_barrier_semaphore()
-    for peer in peers:
-        pl.semaphore_signal(barrier, inc=1, device_id=peer, device_id_type=MESH)
 
     link = Link(send, recv)
     load_p.wait()
@@ -425,20 +421,31 @@
             add_gram(work_g, pl.ds(k * part, part), k == 0)
         yield from gram_total(work_g, into_g, slots_g)
         gram[...] = into_g[...] * (scale_one * scale_one)
-        yield from newton(gram, step, turn_one)
 
     def second_done(k, left):
         add_gram(work_h, split_rows(whole_two, k), left == 3)
 
     panel_total(panel_two, whole_two, rings_two, second_done, first_turn())
 
-    run(gram_total(work_h, into_h, slots_h))
+    def first_applied():
+        yield from newton(gram, turn_one)
+        turn = halves(turn_one[...])
+        for k in range(4):
+            at = pl.ds(k * part, part)
+            y_high[at, :], y_low[at, :] = halves(product((y_high[at, :], y_low[at, :]), turn))
+
+    last_gram, applied = gram_total(work_h, into_h, slots_h), first_applied()
+    next(last_gram)
+    for turn in range(7):
+        next(applied)
+    next(last_gram)
+    run(applied)
+    run(last_gram)
     gram[...] = times(times(turn_one[...], into_h[...]), turn_one[...])
     scale = root_of_trace(gram[...])
     gram[...] = gram[...] * (scale * scale)
-    run(newton(gram, step, turn_two))
-    last = times(turn_one[...], turn_two[...]) * (scale * math.sqrt(D))
-    out[...] = product((y_high[...], y_low[...]), halves(last))
+    run(newton(gram, turn_two))
+    out[...] = product((y_high[...], y_low[...]), halves(turn_two[...] * (scale * math.sqrt(D))))
     link.drain()
 
 
@@ -464,7 +471,7 @@
         + [vm((features, p), F32)] * 4
         + [vm((2 * features, p), F32)] * 2
         + [vm((features, p), F32)]
-        + [vm((p, p), F32)] * 4
+        + [vm((p, p), F32)] * 3
         + [pltpu.SemaphoreType.DMA((280,)), pltpu.SemaphoreType.DMA((280,)), pltpu.SemaphoreType.DMA((1 + 2 * clients,))]
     )
     anywhere = pl.BlockSpec(memory_space=pltpu.MemorySpace.HBM)

time: 128 us -> 130 us (1.016)
  Pallas kernels: 126 us -> 128 us
    pallas_call x1, Pallas kernels: 126 us -> 128 us  [on_device(): pl.pallas_call(kernel, out_shape=jax.ShapeDtypeStruct((features, p), F32)...]
where the time goes in v6:
time: 130 us; the launch traced here: 129 us
  Pallas kernels  128 us (98%)
  local copies, waits for them, and re-layouts  1.63 us (1%)
    pallas_call x1, Pallas kernels, on_device(): pl.pallas_call(kernel, out_shape=jax.ShapeDtypeStruct((features, p), F32)...  128 us

profile of v6, /device:TPU:1, one launch (start us, length us, event | category | flops | bytes accessed | tf_op | source)
XLA Modules:
  0.0 129.5 jit_solution(2682392462356235209)
XLA Ops:
  0.0 0.0 copy-start
  0.0 0.7 copy-done
  0.7 127.8 %shard_map.46 = f32[1024,256]{1,0:T(8,128)S(1)} custom-call(s32[4]{0:T(128)S(1)} %copy-done, f32[4,1024,256]{2,1,0:T(8,128)} %b_hbm.1, f32[4,256,1024]{2,1,0:T(8,128)} %a_hbm.1, f32[1024,256]{1,0:T(8,128)} %p_hbm.1), custom_call_target="tpu_custom_call" | custom-call | tf_op jit(solution)/shard_map/pallas_call | solution.py:478
  128.5 1.0 copy.6
Async XLA Ops:
  0.0 0.7 copy-start

commit v7 on v6

--- a/solution.py
+++ b/solution.py
@@ -419,27 +419,23 @@
     def first_turn():
         for k in range(4):
             add_gram(work_g, pl.ds(k * part, part), k == 0)
-        yield from gram_total(work_g, into_g, slots_g)
+        for leg in gram_total(work_g, into_g, slots_g):
+            for rest in range(4):
+                yield
         gram[...] = into_g[...] * (scale_one * scale_one)
+        yield from newton(gram, turn_one)
 
     def second_done(k, left):
         add_gram(work_h, split_rows(whole_two, k), left == 3)
 
     panel_total(panel_two, whole_two, rings_two, second_done, first_turn())
 
-    def first_applied():
-        yield from newton(gram, turn_one)
-        turn = halves(turn_one[...])
-        for k in range(4):
-            at = pl.ds(k * part, part)
-            y_high[at, :], y_low[at, :] = halves(product((y_high[at, :], y_low[at, :]), turn))
-
-    last_gram, applied = gram_total(work_h, into_h, slots_h), first_applied()
+    last_gram = gram_total(work_h, into_h, slots_h)
     next(last_gram)
-    for turn in range(7):
-        next(applied)
-    next(last_gram)
-    run(applied)
+    turn = halves(turn_one[...])
+    for k in range(4):
+        at = pl.ds(k * part, part)
+        y_high[at, :], y_low[at, :] = halves(product((y_high[at, :], y_low[at, :]), turn))
     run(last_gram)
     gram[...] = times(times(turn_one[...], into_h[...]), turn_one[...])
     scale = root_of_trace(gram[...])

time: 130 us -> 124 us (0.954)
  Pallas kernels: 128 us -> 122 us
    pallas_call x1, Pallas kernels: 128 us -> 122 us  [on_device(): pl.pallas_call(kernel, out_shape=jax.ShapeDtypeStruct((features, p), F32)...]
where the time goes in v7:
time: 124 us
  Pallas kernels  122 us (98%)
  local copies, waits for them, and re-layouts  1.63 us (1%)
    pallas_call x1, Pallas kernels, on_device(): pl.pallas_call(kernel, out_shape=jax.ShapeDtypeStruct((features, p), F32)...  122 us

profile of v7, /device:TPU:1, one launch (start us, length us, event | category | flops | bytes accessed | tf_op | source)
XLA Modules:
  0.0 123.9 jit_solution(3198665982411631326)
XLA Ops:
  0.0 0.0 copy-start
  0.0 0.7 copy-done
  0.7 122.2 %shard_map.46 = f32[1024,256]{1,0:T(8,128)S(1)} custom-call(s32[4]{0:T(128)S(1)} %copy-done, f32[4,1024,256]{2,1,0:T(8,128)} %b_hbm.1, f32[4,256,1024]{2,1,0:T(8,128)} %a_hbm.1, f32[1024,256]{1,0:T(8,128)} %p_hbm.1), custom_call_target="tpu_custom_call" | custom-call | tf_op jit(solution)/shard_map/pallas_call | solution.py:474
  122.9 1.0 copy.6
Async XLA Ops:
  0.0 0.7 copy-start

commit v8 on v7

--- a/solution.py
+++ b/solution.py
@@ -320,13 +320,18 @@
             extent,
         )
 
-    def coef_total(spaces, coef, *others):
+    def coef_total(spaces, coef, early, *others):
         streams = [feat_stream(spaces, k, 2 * rank) for k in range(pairs)]
         for k, c in enumerate(wanted):
             coef(k, c)
             if k < pairs:
                 next(streams[k])
-        run(*streams, *others)
+        for turn in range(3):
+            for stream in (*streams, *others):
+                next(stream, None)
+        run(*others)
+        early()
+        run(*streams)
 
     def first_coef(k, c):
         load_a[k].wait()
@@ -350,11 +355,29 @@
 
     part = features // 4
 
+    def split_coef(coef, chosen, scale=None):
+        for c in chosen:
+            at = pl.ds(pl.multiple_of(c * rank, rank), rank)
+            value = coef[at, :] if scale is None else coef[at, :] * scale
+            c_high[at, :], c_low[at, :] = halves(value)
+
+    def panel_part(work, at, chosen, begin):
+        total = None if begin else work[at, :]
+        for c in chosen:
+            over = pl.ds(pl.multiple_of(c * rank, rank), rank)
+            term = product((b_high[at, over], b_low[at, over]), (c_high[over, :], c_low[over, :]))
+            total = term if total is None else total + term
+        work[at, :] = total
+
+    def panel_begin(work):
+        for k in range(4):
+            panel_part(work, pl.ds(k * part, part), wanted[pairs:], True)
+
     def panel_total(work, into, rings, done, *others):
         streams, open_streams = [], set(range(4))
         for k, kind in enumerate((lower_total, lower_total, upper_total, upper_total)):
             at = pl.ds(k * part, part)
-            work[at, :] = product((b_high[at, :], b_low[at, :]), (c_high[...], c_low[...]))
+            panel_part(work, at, wanted[:pairs], False)
             streams.append(
                 kind(link, place, work, into, rows(rings, 2 * k * part, 2 * part), k * part, part)
             )
@@ -394,8 +417,12 @@
         marks[own, :] = jnp.sum(square.reshape(features // 8, 8, p), axis=0)
         yield from gather_direct(link, marks, 0, place["feat"], 2 * NX, 8, place["along_feat"])
 
-    coef_total(spaces_a, first_coef, b_stream())
-    c_high[...], c_low[...] = halves(into_a[...])
+    def first_early():
+        split_coef(into_a, wanted[pairs:])
+        panel_begin(panel_one)
+
+    coef_total(spaces_a, first_coef, first_early, b_stream())
+    split_coef(into_a, wanted[:pairs])
 
     last_part = []
 
@@ -410,11 +437,19 @@
     panel_total(panel_one, whole_one, rings_one, first_done)
     link.drain()
 
-    coef_total(
-        spaces_b, lambda k, c: client_coef(work_b, c, last_part[0], part, False, True), trace_total()
-    )
-    scale_one = inverse_root(jnp.sum(marks[...], keepdims=True))
-    c_high[...], c_low[...] = halves(into_b[...] * scale_one)
+    def root_one():
+        return inverse_root(jnp.sum(marks[...], keepdims=True))
+
+    def second_early():
+        split_coef(into_b, wanted[pairs:], root_one())
+        panel_begin(panel_two)
+
+    def second_coef(k, c):
+        client_coef(work_b, c, last_part[0], part, False, True)
+
+    coef_total(spaces_b, second_coef, second_early, trace_total())
+    scale_one = root_one()
+    split_coef(into_b, wanted[:pairs], scale_one)
 
     def first_turn():
         for k in range(4):

time: 124 us -> 123 us (level)
  no operation moved by 1% of the time
where the time goes in v8:
time: 123 us
  Pallas kernels  122 us (99%)
  local copies, waits for them, and re-layouts  1.63 us (1%)
    pallas_call x1, Pallas kernels, on_device(): pl.pallas_call(kernel, out_shape=jax.ShapeDtypeStruct((features, p), F32)...  122 us

profile of v8, /device:TPU:1, one launch (start us, length us, event | category | flops | bytes accessed | tf_op | source)
XLA Modules:
  0.0 123.4 jit_solution(4360674630886517721)
XLA Ops:
  0.0 0.0 copy-start
  0.0 0.7 copy-done
  0.7 121.7 %shard_map.46 = f32[1024,256]{1,0:T(8,128)S(1)} custom-call(s32[4]{0:T(128)S(1)} %copy-done, f32[4,1024,256]{2,1,0:T(8,128)} %b_hbm.1, f32[4,256,1024]{2,1,0:T(8,128)} %a_hbm.1, f32[1024,256]{1,0:T(8,128)} %p_hbm.1), custom_call_target="tpu_custom_call" | custom-call | tf_op jit(solution)/shard_map/pallas_call | solution.py:509
  122.4 1.0 copy.6
Async XLA Ops:
  0.0 0.7 copy-start
